TPU v7x, 32 devices: a whole 2x2x4 slice. The times are simulated.
32 devices in a mesh: gx: 4 (over z), gy: 2 (over x), gz: 4 (over y, core).
Axes of the slice: x: 2, y: 2, z: 4, core: 2. Of those that a mesh axis runs over, the one named last changes fastest.
Arguments:
- loads: float32 [4, 2, 4, 1024, 128], P('gx', 'gy', 'gz'), may hold values from -12 to 12
- start: float32 [4, 2, 4, 1024, 128], P('gx', 'gy', 'gz'), may hold values from -6 to 6
- schur: float32 [4, 2, 4, 1024, 1024], P('gx', 'gy', 'gz'), may hold values from -2 to 8
- inv_local: float32 [4, 2, 4, 1024, 1024], P('gx', 'gy', 'gz'), may hold values from -1 to 3
- basis: float32 [4, 2, 4, 1024, 128], P('gx', 'gy', 'gz'), may hold values from -0.1875 to 0.1875
- coarse_inv: float32 [4096, 4096], P(('gx', 'gy')), may hold values from -0.01 to 0.07
- face_index: int32 [4, 2, 4, 6, 160], P('gx', 'gy', 'gz'), may hold values from 0 to 1023, as said below
- multiplicity: int32 [4, 2, 4, 1024], P('gx', 'gy', 'gz'), may hold values from 1 to 2, as said below
- primal_map: int32 [4, 2, 4, 128], P('gx', 'gy', 'gz'), may hold values from 0 to 4095, all different within a row
Outputs:
- solution: float32 [4, 2, 4, 1024, 128], P('gx', 'gy', 'gz')
- residual: float32 [4, 2, 4, 1024, 128], P('gx', 'gy', 'gz')
Inputs may be any that keep to these rules, and one draw needn't show every extreme that they name: face_index[x, y, z, 2a + s] lists 160 distinct interface slots of subdomain (x, y, z) on its face toward the lower (s = 0) or higher (s = 1) neighbour along grid direction a; the six lists of one subdomain are disjoint. `multiplicity`: 1, plus 1 on slots listed in a face whose neighbouring subdomain lies inside the grid. `primal_map`: each subdomain lists 128 distinct primal unknowns, and every primal unknown is listed by some subdomain.
All inputs are finite; a program needn't handle non-finite values.
Results may differ from a plain program's by a relative error of at most 0.00012.
Values sent between devices are 32-bit elements; how exact they have to be, the bound alone decides.
A program may use at most 64 MiB of HBM per device.

v0:
```python
import functools
import itertools

import jax
import jax.numpy as jnp
from jax import lax
from jax.experimental import pallas as pl
from jax.experimental.pallas import tpu as pltpu
from jax.sharding import PartitionSpec as P

ITERS = 2
damping = 0.6
MESH = pl.DeviceIdType.MESH
AXES = ("gx", "gy", "gz")


class Grid:
    def __init__(self, sizes):
        self.sizes = sizes
        gx, gy, gz = sizes
        self.lo = 2 if gz % 2 == 0 else 1
        self.hi = gz // self.lo
        self.stages = (gx, gy, self.hi, self.lo)
        self.count = gx * gy * gz
        self.c = tuple(lax.axis_index(a) for a in AXES)
        self.place = (self.c[0], self.c[1], self.c[2] // self.lo, self.c[2] % self.lo)

    def linear(self, place):
        x, y, h, l = place
        return (x * self.sizes[1] + y) * self.sizes[2] + h * self.lo + l

    def device(self, place):
        x, y, h, l = place
        return (x, y, h * self.lo + l)

    def barrier(self):
        semaphore = pltpu.get_barrier_semaphore()
        total = 0
        for axis in range(3):
            for delta in range(1, self.sizes[axis]):
                target = list(self.c)
                target[axis] = (self.c[axis] + delta) % self.sizes[axis]
                pl.semaphore_signal(
                    semaphore, inc=1, device_id=tuple(target), device_id_type=MESH
                )
                total += 1
        if total:
            pl.semaphore_wait(semaphore, total)


class Gather:
    def __init__(self, grid, buffer, whole, band, order, send, recv):
        self.grid, self.buffer, self.whole, self.band = grid, buffer, whole, band
        self.order, self.send, self.recv = order, send, recv
        self.lengths = tuple(grid.stages[o] for o in order)

    def place(self, offset):
        g = self.grid
        place = list(g.place)
        for o, d in zip(self.order, offset):
            if d:
                place[o] = (g.place[o] + g.stages[o] - d) % g.stages[o]
        return place

    def block(self, offset):
        first = self.grid.linear(self.place(offset)) * self.whole + self.band[0]
        return self.buffer.at[pl.ds(pl.multiple_of(first, 8), self.band[1])]

    def number(self, offset):
        value = 0
        for d, n in zip(offset, self.lengths):
            value = value * n + d
        return value

    def forward(self, offset, first):
        for stage in range(first, 4):
            for delta in range(1, self.lengths[stage]):
                back = [0, 0, 0, 0]
                back[stage] = self.lengths[stage] - delta
                arrived = list(offset)
                arrived[stage] = delta
                k = self.number(arrived)
                block = self.block(offset)
                c = pltpu.make_async_remote_copy(
                    src_ref=block, dst_ref=block, send_sem=self.send,
                    recv_sem=self.recv.at[k], device_id=self.grid.device(self.place(back)),
                    device_id_type=MESH,
                )
                c.start()

    def start(self):
        self.forward((0, 0, 0, 0), 0)

    def finish(self, stage):
        for head in itertools.product(*[range(n) for n in self.lengths[:stage]]):
            for delta in range(1, self.lengths[stage]):
                arrived = tuple(head) + (delta,) + (0,) * (3 - stage)
                block = self.block(arrived)
                k = self.number(arrived)
                pltpu.make_async_remote_copy(
                    src_ref=block, dst_ref=block, send_sem=self.send,
                    recv_sem=self.recv.at[k], device_id=self.grid.c, device_id_type=MESH,
                ).wait_recv()
                self.forward(arrived, stage + 1)

    def drain(self):
        if self.grid.count > 1:
            block = self.buffer.at[pl.ds(0, (self.grid.count - 1) * self.band[1])]
            pltpu.make_async_remote_copy(
                src_ref=block, dst_ref=block, send_sem=self.send, recv_sem=self.recv.at[0],
                device_id=self.grid.c, device_id_type=MESH,
            ).wait_send()


class Halves:
    def __init__(self, grid, buffer, rows, send, recv):
        half = rows // 2
        self.parts = [
            Gather(grid, buffer, rows, (i * half, half), order, send.at[i], recv.at[i])
            for i, order in enumerate(((0, 1, 2, 3), (0, 2, 1, 3)))
        ]

    def start(self):
        for part in self.parts:
            part.start()

    def finish(self):
        for stage in range(4):
            for part in self.parts:
                part.finish(stage)

    def drain(self):
        for part in self.parts:
            part.drain()


def split(value):
    high = value.astype(jnp.bfloat16)
    low = (value - high.astype(jnp.float32)).astype(jnp.bfloat16)
    return high, low


def tile_of(total, want):
    while total % want:
        want //= 2
    return want


def split_rows(source, high, low):
    rows = source.shape[0]
    tile = tile_of(rows, 64)

    def step(i, carry):
        r = pl.ds(pl.multiple_of(i * tile, tile), tile)
        h, l = split(source[r, :])
        high[r, :] = h
        low[r, :] = l
        return carry

    lax.fori_loop(0, rows // tile, step, 0)


def split_beside(source, both):
    rows, width = source.shape
    tile = tile_of(rows, 128)

    def step(i, carry):
        r = pl.ds(pl.multiple_of(i * tile, tile), tile)
        h, l = split(source[r, :])
        both[r, 0:width] = h
        both[r, width : 2 * width] = l
        return carry

    lax.fori_loop(0, rows // tile, step, 0)


def product(high, low, both):
    width = both.shape[1] // 2
    wide = jnp.dot(high, both[...], preferred_element_type=jnp.float32)
    thin = jnp.dot(low, both[:, 0:width], preferred_element_type=jnp.float32)
    return wide[:, 0:width] + wide[:, width:] + thin


def by_rows(rows, want, function):
    tile = tile_of(rows, want)

    def step(i, carry):
        function(pl.ds(pl.multiple_of(i * tile, tile), tile))
        return carry

    lax.fori_loop(0, rows // tile, step, 0)


def take_rows(target, source, index, count, base=0):
    unroll = tile_of(count, 16)

    def step(i, carry):
        first = pl.multiple_of(i * unroll, unroll)
        for j in range(unroll):
            row = index[base, first + j] if len(index.shape) == 2 else index[base + first + j]
            target[pl.ds(first + j, 1), :] = source[pl.ds(row, 1), :]
        return carry

    lax.fori_loop(0, count // unroll, step, 0)


def main_kernel(
    sizes, face,
    slots, places, own_map,
    loads, start, basis, weight, map_block, schur, inverse, coarse_inv,
    solution, residual,
    full, s_high, s_low, b_high, b_low, m_high, m_low, t_high, t_low,
    c_high, c_low, coarse_own, coarse_t, map_all, map_rows, all_map, picked, field, moved, both, term_both, sol_both, coarse_rows,
    faces, arrived, term_all, sol_all,
    load_sem, map_send, map_recv, face_send, face_recv, term_send, term_recv, sol_send, sol_recv,
):
    grid = Grid(sizes)
    unknowns, cases = start.shape
    primal = basis.shape[1]
    own = coarse_t.shape[1]
    local = full.at[:, 0:cases]
    load_s = pltpu.make_async_copy(schur, full, load_sem.at[0])
    load_b = pltpu.make_async_copy(inverse, full, load_sem.at[1])
    load_s.start()
    first_own = pl.multiple_of(grid.c[2] * own, own)
    load_c = pltpu.make_async_copy(coarse_inv.at[pl.ds(first_own, own)], coarse_own, load_sem.at[2])
    load_c.start()
    map_first = pl.multiple_of(grid.linear(grid.place) * 8, 8)
    map_all[pl.ds(map_first, 8), :] = map_block[...]
    for landing in arrived:
        landing[...] = jnp.zeros_like(landing)
    grid.barrier()
    maps = Gather(grid, map_all, 8, (0, 8), (0, 1, 2, 3), map_send, map_recv)
    maps.start()
    split_rows(basis, m_high, m_low)
    for k in range(0, unknowns, primal):
        h, l = split(basis[k : k + primal, :].T)
        t_high[:, k : k + primal] = h
        t_low[:, k : k + primal] = l
    solution[...] = start[...]
    sent = []

    def face_copy(turn, d):
        axis, side = d // 2, d % 2
        target = list(grid.c)
        target[axis] = grid.c[axis] + (1 if side else -1)
        return pltpu.make_async_remote_copy(
            src_ref=faces.at[turn, pl.ds(d * face, face)],
            dst_ref=arrived[turn].at[pl.ds((d ^ 1) * face, face)],
            send_sem=face_send.at[turn, d],
            recv_sem=face_recv.at[turn, d ^ 1],
            device_id=tuple(target), device_id_type=MESH,
        )

    def exists(d):
        axis, side = d // 2, d % 2
        return grid.c[axis] < sizes[axis] - 1 if side else grid.c[axis] > 0

    def exchange_start(turn):
        for d in range(6):
            take_rows(faces.at[turn, pl.ds(d * face, face)], field, slots, face, d * face)

            @pl.when(exists(d))
            def _():
                face_copy(turn, d).start()

    def exchange_finish(turn):
        for d in range(6):

            @pl.when(exists(d))
            def _():
                block = arrived[turn].at[pl.ds(d * face, face)]
                pltpu.make_async_remote_copy(
                    src_ref=block, dst_ref=block, send_sem=face_send.at[turn, d],
                    recv_sem=face_recv.at[turn, d], device_id=grid.c, device_id_type=MESH,
                ).wait_recv()

        take_rows(moved, arrived[turn], places, unknowns)

    def exchange_drain(turn):
        for d in range(6):

            @pl.when(exists(d))
            def _():
                face_copy(turn, d).wait_send()

    gathers = []
    for iteration in range(ITERS):
        turn = 2 * iteration
        split_beside(solution, both)
        if iteration == 0:
            load_s.wait()
            split_rows(full, s_high, s_low)
            load_b.start()
            maps.finish(0)

        def stiff(r):
            field[r, :] = product(s_high[r, :], s_low[r, :], both)

        by_rows(unknowns, 256, stiff)
        if iteration == 0:
            maps.finish(1)
        exchange_start(turn)
        if iteration == 0:
            maps.finish(2)
            load_b.wait()
            split_rows(full, b_high, b_low)

            load_c.wait()
            for k in range(0, coarse_own.shape[1], primal):
                coarse_t[k : k + primal, :] = coarse_own[:, k : k + primal].T
            maps.finish(3)

            def pack(p, carry):
                map_rows[pl.ds(p, 1), :] = map_all[pl.ds(p * 8, 1), :]
                return carry

            lax.fori_loop(0, grid.count, pack, 0)
            to_scalars = pltpu.make_async_copy(map_rows, all_map, load_sem.at[3])
            to_scalars.start()
            to_scalars.wait()

            def pick(p, carry):
                take_rows(picked, coarse_t, all_map, primal, p)
                h, l = split(picked[...].T)
                k = pl.ds(pl.multiple_of(p * primal, primal), primal)
                c_high[:, k] = h
                c_low[:, k] = l
                return carry

            lax.fori_loop(0, grid.count, pick, 0)
        exchange_finish(turn)

        def settle(r):
            value = loads[r, :] - (field[r, :] + moved[r, :])
            residual[r, :] = value
            scaled = weight[r, :] * value
            h, l = split(scaled)
            both[r, 0:cases] = h
            both[r, cases : 2 * cases] = l

        by_rows(unknowns, 128, settle)
        mine = pl.multiple_of(grid.linear(grid.place) * primal, primal)
        term_all[iteration, pl.ds(mine, primal), :] = product(t_high[...], t_low[...], both)
        terms = Halves(grid, term_all.at[iteration], primal, term_send.at[iteration], term_recv.at[iteration])
        terms.start()
        gathers.append(terms)

        def invert(r):
            local[r, :] = product(b_high[r, :], b_low[r, :], both)

        by_rows(unknowns, 256, invert)
        terms.finish()
        mine = pl.multiple_of(grid.linear(grid.place) * own, own)
        coarse_tile = term_both.shape[0]
        sol_all[iteration][pl.ds(mine, own), :] = jnp.zeros((own, cases), jnp.float32)

        def coarse(i, carry):
            k = pl.ds(pl.multiple_of(i * coarse_tile, coarse_tile), coarse_tile)
            split_beside(term_all.at[iteration, k], term_both)
            sol_all[iteration][pl.ds(mine, own), :] += product(c_high[:, k], c_low[:, k], term_both)
            return carry

        lax.fori_loop(0, grid.count * primal // coarse_tile, coarse, 0)
        sols = Halves(grid, sol_all[iteration], own, sol_send.at[iteration], sol_recv.at[iteration])
        sols.start()
        sols.finish()
        gathers.append(sols)
        take_rows(coarse_rows, sol_all[iteration], own_map, primal)
        split_beside(coarse_rows, sol_both)

        def correct(r):
            field[r, :] = weight[r, :] * (local[r, :] + product(m_high[r, :], m_low[r, :], sol_both))

        by_rows(unknowns, 256, correct)
        exchange_start(turn + 1)
        exchange_finish(turn + 1)

        def advance(r):
            solution[r, :] = solution[r, :] + damping * (field[r, :] + moved[r, :])

        by_rows(unknowns, 128, advance)
    for turn in range(2 * ITERS):
        exchange_drain(turn)
    for gather in gathers + [maps]:
        gather.drain()


def places_of(slots, unknowns):
    count = slots.shape[0]
    hit = slots[:, None] == jnp.arange(unknowns, dtype=jnp.int32)[None, :]
    position = jnp.arange(count, dtype=jnp.int32)[:, None] - count
    return jnp.sum(jnp.where(hit, position, 0), axis=0) + count


def body(sizes, loads, start, schur, inv_local, basis, coarse_inv, face_index, multiplicity, primal_map):
    unknowns, cases = loads.shape[3:]
    face = face_index.shape[4]
    primal = basis.shape[4]
    count = sizes[0] * sizes[1] * sizes[2]
    total = coarse_inv.shape[1]
    own = coarse_inv.shape[0] // sizes[2]
    slots = face_index.reshape(-1)
    places = places_of(slots, unknowns)
    own_map = primal_map.reshape(-1)
    vmem = pl.BlockSpec(memory_space=pltpu.VMEM)
    smem = pl.BlockSpec(memory_space=pltpu.SMEM)
    anywhere = pl.BlockSpec(memory_space=pl.ANY)
    dma = pltpu.SemaphoreType.DMA
    weight = jnp.broadcast_to(
        1.0 / multiplicity.reshape(unknowns, 1).astype(jnp.float32), (unknowns, cases)
    )
    modes = basis.reshape(unknowns, primal)
    f32, bf16 = jnp.float32, jnp.bfloat16
    turns = 2 * ITERS
    coarse_tile = tile_of(count * primal, 1024)
    vec = pltpu.VMEM((unknowns, cases), f32)
    out = jax.ShapeDtypeStruct((unknowns, cases), f32)
    solution, residual = pl.pallas_call(
        functools.partial(main_kernel, sizes, face),
        out_shape=(out, out),
        in_specs=[smem] * 3 + [vmem] * 5 + [anywhere] * 3,
        out_specs=(vmem, vmem),
        scratch_shapes=[
            pltpu.VMEM((unknowns, unknowns), f32),
            pltpu.VMEM((unknowns, unknowns), bf16),
            pltpu.VMEM((unknowns, unknowns), bf16),
            pltpu.VMEM((unknowns, unknowns), bf16),
            pltpu.VMEM((unknowns, unknowns), bf16),
            pltpu.VMEM((unknowns, primal), bf16),
            pltpu.VMEM((unknowns, primal), bf16),
            pltpu.VMEM((primal, unknowns), bf16),
            pltpu.VMEM((primal, unknowns), bf16),
            pltpu.VMEM((own, count * primal), bf16),
            pltpu.VMEM((own, count * primal), bf16),
            pltpu.VMEM((own, total), f32),
            pltpu.VMEM((total, own), f32),
            pltpu.VMEM((count * 8, primal), jnp.int32),
            pltpu.VMEM((count, primal), jnp.int32),
            pltpu.SMEM((count, primal), jnp.int32),
            pltpu.VMEM((primal, own), f32),
            vec, vec,
            pltpu.VMEM((unknowns, 2 * cases), bf16),
            pltpu.VMEM((coarse_tile, 2 * cases), bf16),
            pltpu.VMEM((primal, 2 * cases), bf16),
            pltpu.VMEM((primal, cases), f32),
            pltpu.VMEM((turns, 6 * face, cases), f32),
            [pltpu.VMEM((6 * face + 8, cases), f32) for _ in range(turns)],
            pltpu.VMEM((ITERS, count * primal, cases), f32),
            [pltpu.VMEM((total, cases), f32) for _ in range(ITERS)],
            dma((4,)),
            dma(()), dma((count,)),
            dma((turns, 6)), dma((turns, 6)),
            dma((ITERS, 2)), dma((ITERS, 2, count)),
            dma((ITERS, 2)), dma((ITERS, 2, count)),
        ],
        compiler_params=pltpu.CompilerParams(
            collective_id=1, has_side_effects=True, vmem_limit_bytes=67043328
        ),
    )(
        slots, places, own_map,
        loads.reshape(unknowns, cases), start.reshape(unknowns, cases),
        modes, weight, jnp.broadcast_to(own_map[None, :], (8, primal)),
        schur.reshape(unknowns, unknowns), inv_local.reshape(unknowns, unknowns), coarse_inv,
    )
    return (solution.reshape(loads.shape), residual.reshape(loads.shape))


def solution(mesh):
    sizes = tuple(mesh.shape[a] for a in AXES)
    field = P("gx", "gy", "gz", None, None)
    placed = (field,) * 5 + (P(("gx", "gy"), None), field, P("gx", "gy", "gz", None), P("gx", "gy", "gz", None))
    return jax.shard_map(
        functools.partial(body, sizes),
        mesh=mesh,
        in_specs=placed,
        out_specs=(field, field),
        check_vma=False,
    )
```

profile of v0, /device:TPU:1, one launch (start us, length us, event | category | flops | bytes accessed | tf_op | source)
XLA Modules:
  0.0 130.9 jit_solution(10310114344295187711)
XLA Ops:
  0.6 0.7 convert_divide_fusion
  1.3 1.2 broadcast_in_dim.27.map_block
  2.6 0.7 reduce
  3.3 0.1 reshape.51.slots
  3.4 0.0 copy-start
  3.4 0.6 copy-done
  4.0 0.6 select_reduce_fusion
  4.6 0.6 broadcast_add_fusion.places
  5.2 1.0 broadcast_in_dim.26.weight
  6.2 121.0 %shard_map.104 = (f32[1024,128]{1,0:T(8,128)}, f32[1024,128]{1,0:T(8,128)}) custom-call(s32[960]{0:T(1024)} %copy-done, s32[1024]{0:T(1024)} %broadcast_add_fusion.places, s32[128]{0:T(128)} %bitcast.18, f32[1024,128]{1,0:T(8,128)} %bitcast.11, f32[1024,128]{1,0:T(8,128)} %bitcast.12, f32[1024,128]{1,0:T(8,128)} %bitcast.13, ...), custom_call_target="tpu_custom_call" | custom-call | tf_op jit(solution)/shard_map/pallas_call | solution.py:419
  127.2 1.9 %copy.13 = f32[1,1,1,1024,128]{4,3,2,1,0:T(8,128)} copy(f32[1,1,1,1024,128]{4,3,2,1,0:T(8,128)} %bitcast.15) | data formatting | bytes 1048576
  129.0 1.9 %copy.14 = f32[1,1,1,1024,128]{4,3,2,1,0:T(8,128)} copy(f32[1,1,1,1024,128]{4,3,2,1,0:T(8,128)} %bitcast.14) | data formatting | bytes 1048576
  (1 shorter events, 0.0 us)
Async XLA Ops:
  3.4 0.6 copy-start
where the time goes:
time: 132 us; the launch traced here: 131 us
  Pallas kernels  121 us (92%)
  local copies, waits for them, and re-layouts  6.64 us (5%)
  other arithmetic  2.62 us (2%)
    pallas_call x1, Pallas kernels, body(): pl.pallas_call(functools.partial(main_kernel, sizes, face), out_shape=(ou...  121 us
    unnamed x4, local copies, waits for them, and re-layouts  4.33 us

commit v1 on v0

v1 whole, which is shorter than its diff:
```python
import functools
import itertools

import jax
import jax.numpy as jnp
from jax import lax
from jax.experimental import pallas as pl
from jax.experimental.pallas import tpu as pltpu
from jax.sharding import PartitionSpec as P

ITERS = 2
damping = 0.6
MESH = pl.DeviceIdType.MESH
AXES = ("gx", "gy", "gz")


class Grid:
    def __init__(self, sizes):
        self.sizes = sizes
        gx, gy, gz = sizes
        self.lo = 2 if gz % 2 == 0 else 1
        self.hi = gz // self.lo
        self.stages = (gx, gy, self.hi, self.lo)
        self.count = gx * gy * gz
        self.c = tuple(lax.axis_index(a) for a in AXES)
        self.place = (self.c[0], self.c[1], self.c[2] // self.lo, self.c[2] % self.lo)

    def linear(self, place):
        x, y, h, l = place
        return (x * self.sizes[1] + y) * self.sizes[2] + h * self.lo + l

    def device(self, place):
        x, y, h, l = place
        return (x, y, h * self.lo + l)

    def others(self, function):
        gx, gy, gz = self.sizes
        me = self.linear(self.place)

        def step(delta, carry):
            t = (me + delta) % self.count
            function((t // (gy * gz), (t // gz) % gy, t % gz))
            return carry

        lax.fori_loop(1, self.count, step, 0)

    def announce(self):
        semaphore = pltpu.get_barrier_semaphore()
        self.others(
            lambda target: pl.semaphore_signal(
                semaphore, inc=1, device_id=target, device_id_type=MESH
            )
        )

    def meet(self):
        if self.count > 1:
            pl.semaphore_wait(pltpu.get_barrier_semaphore(), self.count - 1)


class Gather:
    def __init__(self, grid, buffer, whole, band, order, send, recv):
        self.grid, self.buffer, self.whole, self.band = grid, buffer, whole, band
        self.order, self.send, self.recv = order, send, recv
        self.lengths = tuple(grid.stages[o] for o in order)

    def place(self, offset):
        g = self.grid
        place = list(g.place)
        for o, d in zip(self.order, offset):
            if d:
                place[o] = (g.place[o] + g.stages[o] - d) % g.stages[o]
        return place

    def block(self, offset):
        first = self.grid.linear(self.place(offset)) * self.whole + self.band[0]
        return self.buffer.at[pl.ds(pl.multiple_of(first, 8), self.band[1])]

    def number(self, offset):
        value = 0
        for d, n in zip(offset, self.lengths):
            value = value * n + d
        return value

    def forward(self, offset, first):
        for stage in range(first, 4):
            for delta in range(1, self.lengths[stage]):
                back = [0, 0, 0, 0]
                back[stage] = self.lengths[stage] - delta
                arrived = list(offset)
                arrived[stage] = delta
                k = self.number(arrived)
                block = self.block(offset)
                c = pltpu.make_async_remote_copy(
                    src_ref=block, dst_ref=block, send_sem=self.send,
                    recv_sem=self.recv.at[k], device_id=self.grid.device(self.place(back)),
                    device_id_type=MESH,
                )
                c.start()

    def start(self):
        self.forward((0, 0, 0, 0), 0)

    def finish(self, stage):
        for head in itertools.product(*[range(n) for n in self.lengths[:stage]]):
            for delta in range(1, self.lengths[stage]):
                arrived = tuple(head) + (delta,) + (0,) * (3 - stage)
                block = self.block(arrived)
                k = self.number(arrived)
                pltpu.make_async_remote_copy(
                    src_ref=block, dst_ref=block, send_sem=self.send,
                    recv_sem=self.recv.at[k], device_id=self.grid.c, device_id_type=MESH,
                ).wait_recv()
                self.forward(arrived, stage + 1)

    def drain(self):
        if self.grid.count > 1:
            block = self.buffer.at[pl.ds(0, (self.grid.count - 1) * self.band[1])]
            pltpu.make_async_remote_copy(
                src_ref=block, dst_ref=block, send_sem=self.send, recv_sem=self.recv.at[0],
                device_id=self.grid.c, device_id_type=MESH,
            ).wait_send()


class Halves:
    def __init__(self, grid, buffer, rows, send, recv):
        half = rows // 2
        self.parts = [
            Gather(grid, buffer, rows, (i * half, half), order, send.at[i], recv.at[i])
            for i, order in enumerate(((0, 1, 2, 3), (0, 2, 1, 3)))
        ]

    def start(self):
        for part in self.parts:
            part.start()

    def finish(self, work=()):
        work = list(work)
        for stage in range(4):
            for part in self.parts:
                part.finish(stage)
                if work:
                    work.pop(0)()
        for rest in work:
            rest()

    def drain(self):
        for part in self.parts:
            part.drain()


def split(value):
    high = value.astype(jnp.bfloat16)
    low = (value - high.astype(jnp.float32)).astype(jnp.bfloat16)
    return high, low


def tile_of(total, want):
    while total % want:
        want //= 2
    return want


def split_rows(source, high, low):
    rows = source.shape[0]
    tile = tile_of(rows, 64)

    def step(i, carry):
        r = pl.ds(pl.multiple_of(i * tile, tile), tile)
        h, l = split(source[r, :])
        high[r, :] = h
        low[r, :] = l
        return carry

    lax.fori_loop(0, rows // tile, step, 0)


def split_beside(source, both):
    rows, width = source.shape
    tile = tile_of(rows, 128)

    def step(i, carry):
        r = pl.ds(pl.multiple_of(i * tile, tile), tile)
        h, l = split(source[r, :])
        both[r, 0:width] = h
        both[r, width : 2 * width] = l
        return carry

    lax.fori_loop(0, rows // tile, step, 0)


def product(high, low, both):
    width = both.shape[1] // 2
    wide = jnp.dot(high, both[...], preferred_element_type=jnp.float32)
    thin = jnp.dot(low, both[:, 0:width], preferred_element_type=jnp.float32)
    return wide[:, 0:width] + wide[:, width:] + thin


def by_rows(rows, want, function):
    tile = tile_of(rows, want)

    def step(i, carry):
        function(pl.ds(pl.multiple_of(i * tile, tile), tile))
        return carry

    lax.fori_loop(0, rows // tile, step, 0)


def take_rows(target, source, index, count):
    unroll = tile_of(count, 32)

    def step(i, carry):
        first = pl.multiple_of(i * unroll, unroll)
        for j in range(unroll):
            target[pl.ds(first + j, 1), :] = source[pl.ds(index(first + j), 1), :]
        return carry

    lax.fori_loop(0, count // unroll, step, 0)


def main_kernel(
    sizes, face,
    slots, slot_rows, multiplicity, own_map,
    loads_in, start_in, basis_in, schur, inverse, coarse_inv,
    solution_out, residual_out,
    full, s_high, s_low, b_high, b_low, m_high, m_low, t_high, t_low, p_high, p_low, n_high, n_low,
    c_high, c_low, coarse_own, coarse_t, map_all, all_map, picked, spread,
    loads, solution, basis, weight, residual, field, local, early, both, edge_both, term_both, sol_both, coarse_rows, corrected,
    faces, arrived, term_all, sol_all,
    load_sem, out_sem, map_send, map_recv, face_send, face_recv, term_send, term_recv, sol_send, sol_recv,
):
    grid = Grid(sizes)
    unknowns, cases = solution.shape
    primal = basis.shape[1]
    own = coarse_t.shape[1]
    edge = corrected.shape[0]
    shape_turn = 2 * ITERS
    first_own = pl.multiple_of(grid.c[2] * own, own)

    def load(k, source, target):
        return pltpu.make_async_copy(source, target, load_sem.at[k])

    load_x = load(0, start_in, solution)
    load_s = load(1, schur, full)
    load_m = load(2, basis_in, basis)
    load_l = load(3, loads_in, loads)
    load_c = load(4, coarse_inv.at[pl.ds(first_own, own)], coarse_own)
    load_b = load(5, inverse, full)
    for each in (load_x, load_s, load_m, load_l, load_c):
        each.start()
    for landing in arrived:
        landing[...] = jnp.zeros_like(landing)
    with jax.named_scope("announce"):
        grid.announce()

    me = grid.linear(grid.place)
    map_all[me] = own_map[...]

    with jax.named_scope("splitx"):
        load_x.wait()
        split_beside(solution, both)
    with jax.named_scope("waits"):
        load_s.wait()
    with jax.named_scope("splits"):
        split_rows(full, s_high, s_low)
    load_b.start()

    def stiff(r):
        field[r, :] = product(s_high[r, :], s_low[r, :], both)

    with jax.named_scope("stiff"):
        by_rows(unknowns, 256, stiff)

    def face_copy(turn, d):
        axis, side = d // 2, d % 2
        target = list(grid.c)
        target[axis] = grid.c[axis] + (1 if side else -1)
        return pltpu.make_async_remote_copy(
            src_ref=faces.at[turn, pl.ds(d * face, face)],
            dst_ref=arrived[turn].at[pl.ds((d ^ 1) * face, face)],
            send_sem=face_send.at[turn, d],
            recv_sem=face_recv.at[turn, d ^ 1],
            device_id=tuple(target), device_id_type=MESH,
        )

    def exists(d):
        axis, side = d // 2, d % 2
        return grid.c[axis] < sizes[axis] - 1 if side else grid.c[axis] > 0

    def collect(turn, source, d):
        take_rows(faces.at[turn, pl.ds(d * face, face)], source, lambda k: slots[d, k], face)

    def dispatch(turn, d):
        @pl.when(exists(d))
        def _():
            face_copy(turn, d).start()

    def exchange_start(turn, source):
        for d in range(6):
            collect(turn, source, d)
            dispatch(turn, d)

    def exchange_wait(turn):
        for d in range(6):

            @pl.when(exists(d))
            def _():
                block = arrived[turn].at[pl.ds(d * face, face)]
                pltpu.make_async_remote_copy(
                    src_ref=block, dst_ref=block, send_sem=face_send.at[turn, d],
                    recv_sem=face_recv.at[turn, d], device_id=grid.c, device_id_type=MESH,
                ).wait_recv()

    def exchange_drain(turn):
        for d in range(6):

            @pl.when(exists(d))
            def _():
                face_copy(turn, d).wait_send()

    with jax.named_scope("basis"):
        load_m.wait()
        for k in range(0, unknowns, 128):
            r = slice(k, k + 128)
            inverse_count = 1.0 / multiplicity[:, r].astype(jnp.float32)
            weight[r, :] = jnp.broadcast_to(inverse_count, (cases, 128)).T
            scaled = weight[r, 0:1] * basis[r, :]
            basis[r, :] = scaled
            h, l = split(scaled)
            m_high[r, :] = h
            m_low[r, :] = l
            h, l = split(scaled.T)
            t_high[:, r] = h
            t_low[:, r] = l
    with jax.named_scope("collect0"):
        for d in range(6):
            collect(0, field, d)
    with jax.named_scope("psi"):
        shape_edges = faces.at[shape_turn]
        for d in range(6):
            collect(shape_turn, basis, d)
        if edge > 6 * face:
            shape_edges[6 * face : edge, :] = jnp.zeros((edge - 6 * face, cases), jnp.float32)
        for k in range(0, edge, 128):
            h, l = split(shape_edges[k : k + 128, :].T)
            p_high[:, k : k + 128] = h
            p_low[:, k : k + 128] = l
    with jax.named_scope("meet"):
        grid.meet()
    with jax.named_scope("dispatch"):
        for d in range(6):
            dispatch(0, d)
        for d in range(6):
            dispatch(shape_turn, d)

        def map_copy(target):
            return pltpu.make_async_remote_copy(
                src_ref=map_all.at[me], dst_ref=map_all.at[me], send_sem=map_send, recv_sem=map_recv,
                device_id=target, device_id_type=MESH,
            )

        grid.others(lambda target: map_copy(target).start())
    with jax.named_scope("spread"):
        hits = slot_rows[...]
        tile = tile_of(unknowns, 64)

        def mark(i, carry):
            r = pl.ds(pl.multiple_of(i * tile, tile), tile)
            row = lax.broadcasted_iota(jnp.int32, (tile, edge), 0) + i * tile
            spread[r, :] = jnp.where(row == hits, 1.0, 0.0).astype(jnp.bfloat16)
            return carry

        lax.fori_loop(0, unknowns // tile, mark, 0)
        corrected[...] = jnp.zeros_like(corrected)

    def moved(r):
        wide = jnp.dot(spread[r, :], edge_both[...], preferred_element_type=jnp.float32)
        return wide[:, 0:cases] + wide[:, cases : 2 * cases]

    def neighbour(d):
        axis, side = d // 2, d % 2
        stride = (sizes[1] * sizes[2], sizes[2], 1)[axis]
        step = (grid.c[axis] + (1 if side else -1) + sizes[axis]) % sizes[axis] - grid.c[axis]
        return me + step * stride

    gathers = []
    for iteration in range(ITERS):
        turn = 2 * iteration
        slot = iteration % term_all.shape[0]
        if slot < iteration:
            gathers.pop(0).drain()
        if iteration:
            with jax.named_scope("splitx"):
                split_beside(solution, both)
            with jax.named_scope("stiff"):
                by_rows(unknowns, 256, stiff)
            with jax.named_scope("xstart"):
                exchange_start(turn, field)
        else:
            load_l.wait()

        def before(r):
            value = loads[r, :] - field[r, :]
            field[r, :] = value
            h, l = split(value)
            both[r, 0:cases] = h
            both[r, cases : 2 * cases] = l

        with jax.named_scope("before"):
            by_rows(unknowns, 128, before)
            early[...] = product(t_high[...], t_low[...], both)
        if iteration == 0:
            with jax.named_scope("splitb"):
                load_b.wait()
                split_rows(full, b_high, b_low)
            with jax.named_scope("transc"):
                load_c.wait()
                for k in range(0, coarse_own.shape[1], 128):
                    coarse_t[k : k + 128, :] = coarse_own[:, k : k + 128].T
        with jax.named_scope("xwait"):
            exchange_wait(turn)
        with jax.named_scope("term"):
            split_beside(arrived[turn], edge_both)
            mine = pl.multiple_of(me * primal, primal)
            term_all[slot, pl.ds(mine, primal), :] = early[...] - product(p_high[...], p_low[...], edge_both)
        terms = Halves(grid, term_all.at[slot], primal, term_send.at[iteration], term_recv.at[iteration])
        with jax.named_scope("termstart"):
            terms.start()
        gathers.append(terms)

        def settle(r):
            value = field[r, :] - moved(r)
            residual[r, :] = value
            h, l = split(weight[r, :] * value)
            both[r, 0:cases] = h
            both[r, cases : 2 * cases] = l

        with jax.named_scope("settle"):
            by_rows(unknowns, 256, settle)
        if iteration == ITERS - 1:
            out_residual = pltpu.make_async_copy(residual, residual_out, out_sem.at[0])
            out_residual.start()

        def invert(r):
            local[r, :] = weight[r, :] * product(b_high[r, :], b_low[r, :], both)

        with jax.named_scope("invert"):
            by_rows(unknowns, 256, invert)
        with jax.named_scope("xlocal"):
            exchange_start(turn + 1, local)

        def read_maps():
            with jax.named_scope("maps"):
                if grid.count > 1:
                    block = map_all.at[pl.ds(0, grid.count - 1)]
                    pltpu.make_async_remote_copy(
                        src_ref=block, dst_ref=block, send_sem=map_send, recv_sem=map_recv,
                        device_id=grid.c, device_id_type=MESH,
                    ).wait()
                to_scalars = pltpu.make_async_copy(map_all, all_map, load_sem.at[6])
                to_scalars.start()
                to_scalars.wait()

        def pick(p, carry):
            take_rows(picked, coarse_t, lambda k: all_map[p, 0, k], primal)
            h, l = split(picked[...].T)
            k = pl.ds(pl.multiple_of(p * primal, primal), primal)
            c_high[:, k] = h
            c_low[:, k] = l
            return carry

        def picks(lower, upper):
            def run():
                with jax.named_scope("pick"):
                    lax.fori_loop(lower, upper, pick, 0)

            return run

        def shapes():
            with jax.named_scope("shapes"):
                exchange_wait(shape_turn)
                split_rows(arrived[shape_turn], n_high, n_low)

        work = []
        if iteration == 0:
            parts = 4
            bounds = [grid.count * k // parts for k in range(parts + 1)]
            work = [read_maps] + [picks(bounds[k], bounds[k + 1]) for k in range(parts)] + [shapes]
        with jax.named_scope("termfin"):
            terms.finish(work)
        mine = pl.multiple_of(me * own, own)
        coarse_tile = term_both.shape[0]
        sol_all[iteration][pl.ds(mine, own), :] = jnp.zeros((own, cases), jnp.float32)

        def coarse(i, carry):
            k = pl.ds(pl.multiple_of(i * coarse_tile, coarse_tile), coarse_tile)
            split_beside(term_all.at[slot, k], term_both)
            sol_all[iteration][pl.ds(mine, own), :] += product(c_high[:, k], c_low[:, k], term_both)
            return carry

        with jax.named_scope("coarse"):
            lax.fori_loop(0, grid.count * primal // coarse_tile, coarse, 0)
        sols = Halves(grid, sol_all[iteration], own, sol_send.at[iteration], sol_recv.at[iteration])
        with jax.named_scope("solstart"):
            sols.start()
        gathers.append(sols)

        with jax.named_scope("xlwait"):
            exchange_wait(turn + 1)

        def approach(r):
            solution[r, :] = solution[r, :] + damping * (local[r, :] + moved(r))

        with jax.named_scope("approach"):
            split_beside(arrived[turn + 1], edge_both)
            by_rows(unknowns, 256, approach)
        with jax.named_scope("solfin"):
            sols.finish()
        with jax.named_scope("take"):
            take_rows(coarse_rows, sol_all[iteration], lambda k: all_map[me, 0, k], primal)
            split_beside(coarse_rows, sol_both)
            for d in range(6):
                q = neighbour(d)
                r = slice(d * face, (d + 1) * face)
                take_rows(coarse_rows, sol_all[iteration], lambda k: all_map[q, 0, k], primal)
                split_beside(coarse_rows, term_both.at[0:primal])
                corrected[r, :] = product(n_high[r, :], n_low[r, :], term_both.at[0:primal])
            split_beside(corrected, edge_both)

        def advance(r):
            change = product(m_high[r, :], m_low[r, :], sol_both) + moved(r)
            solution[r, :] = solution[r, :] + damping * change

        with jax.named_scope("advance"):
            by_rows(unknowns, 256, advance)
    with jax.named_scope("out"):
        out_solution = pltpu.make_async_copy(solution, solution_out, out_sem.at[1])
        out_solution.start()
        for turn in range(2 * ITERS + 1):
            exchange_drain(turn)
        for gather in gathers:
            gather.drain()
        out_residual.wait()
        out_solution.wait()


def body(sizes, loads, start, schur, inv_local, basis, coarse_inv, face_index, multiplicity, primal_map):
    unknowns, cases = loads.shape[3:]
    face = face_index.shape[4]
    primal = basis.shape[4]
    count = sizes[0] * sizes[1] * sizes[2]
    total = coarse_inv.shape[1]
    own = coarse_inv.shape[0] // sizes[2]
    edge = -(-6 * face // 128) * 128
    vmem = pl.BlockSpec(memory_space=pltpu.VMEM)
    smem = pl.BlockSpec(memory_space=pltpu.SMEM)
    anywhere = pl.BlockSpec(memory_space=pl.ANY)
    dma = pltpu.SemaphoreType.DMA
    f32, bf16 = jnp.float32, jnp.bfloat16
    turns = 2 * ITERS + 1
    coarse_tile = tile_of(count * primal, 1024)
    term_slots = ITERS if ITERS * count * primal <= 8 * unknowns else 1
    vec = pltpu.VMEM((unknowns, cases), f32)
    out = jax.ShapeDtypeStruct((unknowns, cases), f32)
    lists = face_index.reshape(6, face)
    row = jnp.pad(lists.reshape(1, 6 * face), ((0, 0), (0, edge - 6 * face)), constant_values=-1)
    solution, residual = pl.pallas_call(
        functools.partial(main_kernel, sizes, face),
        out_shape=(out, out),
        in_specs=[smem] + [vmem] * 3 + [anywhere] * 6,
        out_specs=(anywhere, anywhere),
        scratch_shapes=[
            pltpu.VMEM((unknowns, unknowns), f32),
            pltpu.VMEM((unknowns, unknowns), bf16),
            pltpu.VMEM((unknowns, unknowns), bf16),
            pltpu.VMEM((unknowns, unknowns), bf16),
            pltpu.VMEM((unknowns, unknowns), bf16),
            pltpu.VMEM((unknowns, primal), bf16),
            pltpu.VMEM((unknowns, primal), bf16),
            pltpu.VMEM((primal, unknowns), bf16),
            pltpu.VMEM((primal, unknowns), bf16),
            pltpu.VMEM((primal, edge), bf16),
            pltpu.VMEM((primal, edge), bf16),
            pltpu.VMEM((edge, primal), bf16),
            pltpu.VMEM((edge, primal), bf16),
            pltpu.VMEM((own, count * primal), bf16),
            pltpu.VMEM((own, count * primal), bf16),
            pltpu.VMEM((own, total), f32),
            pltpu.VMEM((total, own), f32),
            pltpu.VMEM((count, 1, primal), jnp.int32),
            pltpu.SMEM((count, 1, primal), jnp.int32),
            pltpu.VMEM((primal, own), f32),
            pltpu.VMEM((unknowns, edge), bf16),
            vec, vec, pltpu.VMEM((unknowns, primal), f32), vec, vec, vec, vec,
            pltpu.VMEM((primal, cases), f32),
            pltpu.VMEM((unknowns, 2 * cases), bf16),
            pltpu.VMEM((edge, 2 * cases), bf16),
            pltpu.VMEM((coarse_tile, 2 * cases), bf16),
            pltpu.VMEM((primal, 2 * cases), bf16),
            pltpu.VMEM((primal, cases), f32),
            pltpu.VMEM((edge, cases), f32),
            pltpu.VMEM((turns, edge, cases), f32),
            [pltpu.VMEM((edge, cases), f32) for _ in range(turns)],
            pltpu.VMEM((term_slots, count * primal, cases), f32),
            [pltpu.VMEM((total, cases), f32) for _ in range(ITERS)],
            dma((7,)), dma((2,)),
            dma(()), dma(()),
            dma((turns, 6)), dma((turns, 6)),
            dma((ITERS, 2)), dma((ITERS, 2, count)),
            dma((ITERS, 2)), dma((ITERS, 2, count)),
        ],
        compiler_params=pltpu.CompilerParams(
            collective_id=1, has_side_effects=True, vmem_limit_bytes=67043328
        ),
    )(
        lists, row, multiplicity.reshape(1, unknowns), primal_map.reshape(1, primal),
        loads.reshape(unknowns, cases), start.reshape(unknowns, cases), basis.reshape(unknowns, primal),
        schur.reshape(unknowns, unknowns), inv_local.reshape(unknowns, unknowns), coarse_inv,
    )
    return (solution.reshape(loads.shape), residual.reshape(loads.shape))


def solution(mesh):
    sizes = tuple(mesh.shape[a] for a in AXES)
    field = P("gx", "gy", "gz", None, None)
    placed = (field,) * 5 + (P(("gx", "gy"), None), field, P("gx", "gy", "gz", None), P("gx", "gy", "gz", None))
    return jax.shard_map(
        functools.partial(body, sizes),
        mesh=mesh,
        in_specs=placed,
        out_specs=(field, field),
        check_vma=False,
    )
```

time: 132 us -> 118 us (0.89)
  Pallas kernels: 121 us -> 111 us
  other arithmetic: 2.62 us -> 0.72 us
    pallas_call x1, Pallas kernels: 121 us -> 111 us  [body(): pl.pallas_call(functools.partial(main_kernel, sizes, face), out_shape=(ou...]
    broadcast_in_dim x2 -> x0, local copies, waits for them, and re-layouts: 2.24 us -> none  [the longest x1 1.25 us: body(): jnp.broadcast_to(own_map[None, :], (8, primal))]
    unnamed x4 -> x3, local copies, waits for them, and re-layouts: 4.33 us -> 5.03 us
where the time goes in v1:
time: 118 us
  Pallas kernels  111 us (94%)
  local copies, waits for them, and re-layouts  5.71 us (5%)
    pallas_call x1, Pallas kernels, body(): pl.pallas_call(functools.partial(main_kernel, sizes, face), out_shape=(ou...  111 us
    unnamed x3, local copies, waits for them, and re-layouts  5.03 us

profile of v1, /device:TPU:1, one launch (start us, length us, event | category | flops | bytes accessed | tf_op | source)
XLA Modules:
  0.0 117.8 jit_solution(371575684776105346)
XLA Ops:
  0.6 0.7 reduce
  1.3 0.1 reshape_reshape.3
  1.4 0.6 pad.4.slot_rows
  2.0 1.3 %copy.13 = s32[1,1,1,6,160]{4,3,2,1,0:T(8,128)} copy(s32[1,1,1,6,160]{4,2,3,1,0:T(1,128)} %param.15) | data formatting | bytes 7680
  3.3 110.7 %shard_map.104 = (f32[1024,128]{1,0:T(8,128)}, f32[1024,128]{1,0:T(8,128)}) custom-call(s32[6,160]{1,0:T(8,128)} %bitcast.19, s32[1,1024]{1,0:T(1,128)} %pad.4.slot_rows, s32[1,1024]{1,0:T(1,128)} %bitcast.20, s32[1,128]{1,0:T(1,128)} %bitcast.21, f32[1024,128]{1,0:T(8,128)} %bitcast.14, f32[1024,128]{1,0:T(8,128)} %bitcast.15, f32[1024,128]{1,0:T(8,128)} %bitcast.16, ...), custom_call_target="tpu_custom_call" | custom-call | tf_op jit(solution)/shard_map/pallas_call | solution.py:566
  114.0 1.9 %copy.16 = f32[1,1,1,1024,128]{4,3,2,1,0:T(8,128)} copy(f32[1,1,1,1024,128]{4,3,2,1,0:T(8,128)} %bitcast.18) | data formatting | bytes 1048576
  115.9 1.9 %copy.17 = f32[1,1,1,1024,128]{4,3,2,1,0:T(8,128)} copy(f32[1,1,1,1024,128]{4,3,2,1,0:T(8,128)} %bitcast.17) | data formatting | bytes 1048576

commit v2 on v1

v2 whole, which is shorter than its diff:
```python
import functools
import itertools

import jax
import jax.numpy as jnp
from jax import lax
from jax.experimental import pallas as pl
from jax.experimental.pallas import tpu as pltpu
from jax.sharding import PartitionSpec as P

ITERS = 2
damping = 0.6
MESH = pl.DeviceIdType.MESH
AXES = ("gx", "gy", "gz")


def stages_of(sizes):
    gx, gy, gz = sizes
    lo = 2 if gz % 2 == 0 else 1
    return (gx, gy, gz // lo, lo)


class Grid:
    def __init__(self, sizes):
        self.sizes = sizes
        gx, gy, gz = sizes
        self.stages = stages_of(sizes)
        self.hi, self.lo = self.stages[2:]
        self.count = gx * gy * gz
        self.c = tuple(lax.axis_index(a) for a in AXES)
        self.place = (self.c[0], self.c[1], self.c[2] // self.lo, self.c[2] % self.lo)

    def linear(self, place):
        x, y, h, l = place
        return (x * self.sizes[1] + y) * self.sizes[2] + h * self.lo + l

    def device(self, place):
        x, y, h, l = place
        return (x, y, h * self.lo + l)

    def others(self, function):
        along = [[(c + d) % n for d in range(n)] for c, n in zip(self.c, self.sizes)]
        for target in list(itertools.product(*along))[1:]:
            function(target)

    def announce(self):
        semaphore = pltpu.get_barrier_semaphore()
        self.others(
            lambda target: pl.semaphore_signal(
                semaphore, inc=1, device_id=target, device_id_type=MESH
            )
        )

    def meet(self):
        if self.count > 1:
            pl.semaphore_wait(pltpu.get_barrier_semaphore(), self.count - 1)


class Gather:
    def __init__(self, grid, buffer, whole, band, order, send, recv):
        self.grid, self.buffer, self.whole, self.band = grid, buffer, whole, band
        self.order, self.send, self.recv = order, send, recv
        self.lengths = tuple(grid.stages[o] for o in order)

    def place(self, offset):
        g = self.grid
        place = list(g.place)
        for o, d in zip(self.order, offset):
            if d:
                place[o] = (g.place[o] + g.stages[o] - d) % g.stages[o]
        return place

    def block(self, offset):
        first = self.grid.linear(self.place(offset)) * self.whole + self.band[0]
        return self.buffer.at[pl.ds(pl.multiple_of(first, 8), self.band[1])]

    def number(self, offset):
        if offset[3]:
            return arrivals(self.lengths) - self.lengths[0] + offset[0]
        value = 0
        for d, n in zip(offset[:3], self.lengths[:3]):
            value = value * n + d
        return value - 1

    def copy(self, block, k, target):
        return pltpu.make_async_remote_copy(
            src_ref=block, dst_ref=block, send_sem=self.send, recv_sem=self.recv.at[k],
            device_id=target, device_id_type=MESH,
        )

    def forward(self, offset, first):
        for stage in range(first, 4):
            for delta in range(1, self.lengths[stage]):
                back = [0, 0, 0, 0]
                back[stage] = self.lengths[stage] - delta
                arrived = list(offset)
                arrived[stage] = delta
                self.copy(
                    self.block(offset), self.number(arrived), self.grid.device(self.place(back))
                ).start()

    def start(self):
        self.forward((0, 0, 0, 0), 0)

    def finish(self, stage, heads=None, idle=None):
        for head in itertools.product(*[range(n) for n in self.lengths[:stage]]):
            if heads is not None and head[0] != heads:
                continue
            for delta in range(1, self.lengths[stage]):
                arrived = tuple(head) + (delta,) + (0,) * (3 - stage)
                self.copy(self.block(arrived), self.number(arrived), self.grid.c).wait_recv()
                self.forward(arrived, stage + 1)
                if idle:
                    idle()

    def close(self, head):
        n = self.lengths
        rows = n[1] * n[2] * (n[3] - 1) * self.band[1]
        if rows:
            block = self.buffer.at[pl.ds(0, rows)]
            self.copy(block, self.number((head, 0, 0, 1)), self.grid.c).wait_recv()

    def drain(self):
        if self.grid.count > 1:
            block = self.buffer.at[pl.ds(0, (self.grid.count - 1) * self.band[1])]
            self.copy(block, 0, self.grid.c).wait_send()


def arrivals(lengths):
    return lengths[0] * lengths[1] * lengths[2] - 1 + lengths[0]


class Halves:
    def __init__(self, grid, buffer, rows, send, recv):
        half = rows // 2
        self.heads = grid.stages[0]
        self.parts = [
            Gather(grid, buffer, rows, (i * half, half), order, send.at[i], recv.at[i])
            for i, order in enumerate(((0, 1, 2, 3), (0, 2, 1, 3)))
        ]

    def start(self):
        for part in self.parts:
            part.start()

    def finish(self, first=(), work=(), after=None):
        first, work = list(first), list(work)

        def idle():
            if first or work:
                (first or work).pop(0)()

        for stage in range(2):
            for part in self.parts:
                part.finish(stage, None, idle)

        def close(head):
            for part in self.parts:
                part.close(head)
            while first:
                idle()
            if after:
                after(head)

        for head in range(self.heads):
            for part in self.parts:
                part.finish(2, head, idle)
            if head:
                close(head - 1)
        while first or work:
            idle()
        close(self.heads - 1)

    def drain(self):
        for part in self.parts:
            part.drain()


def split(value):
    high = value.astype(jnp.bfloat16)
    low = (value - high.astype(jnp.float32)).astype(jnp.bfloat16)
    return high, low


def tile_of(total, want):
    while total % want:
        want //= 2
    return want


def split_rows(source, high, low):
    rows = source.shape[0]
    tile = tile_of(rows, 64)

    def step(i, carry):
        r = pl.ds(pl.multiple_of(i * tile, tile), tile)
        h, l = split(source[r, :])
        high[r, :] = h
        low[r, :] = l
        return carry

    lax.fori_loop(0, rows // tile, step, 0)


def split_beside(source, both):
    rows, width = source.shape
    tile = tile_of(rows, 128)

    def step(i, carry):
        r = pl.ds(pl.multiple_of(i * tile, tile), tile)
        h, l = split(source[r, :])
        both[r, 0:width] = h
        both[r, width : 2 * width] = l
        return carry

    lax.fori_loop(0, rows // tile, step, 0)


def product(high, low, both):
    width = both.shape[1] // 2
    wide = jnp.dot(high, both[...], preferred_element_type=jnp.float32)
    thin = jnp.dot(low, both[:, 0:width], preferred_element_type=jnp.float32)
    return wide[:, 0:width] + wide[:, width:] + thin


def by_rows(rows, want, function):
    tile = tile_of(rows, want)

    def step(i, carry):
        function(pl.ds(pl.multiple_of(i * tile, tile), tile))
        return carry

    lax.fori_loop(0, rows // tile, step, 0)


def take_rows(target, source, index, count):
    unroll = tile_of(count, 32)

    def step(i, carry):
        first = pl.multiple_of(i * unroll, unroll)
        for j in range(unroll):
            target[pl.ds(first + j, 1), :] = source[pl.ds(index[first + j], 1), :]
        return carry

    lax.fori_loop(0, count // unroll, step, 0)


def main_kernel(
    sizes, face,
    lists_in, multiplicity_in, own_map_in,
    loads_in, start_in, basis_in, schur, inverse, coarse_inv,
    solution_out, residual_out,
    slots, slot_lists, multiplicity, full, s_high, s_low, b_high, b_low, m_high, m_low, t_high, t_low, p_high, p_low, n_high, n_low,
    c_high, c_low, coarse_own, coarse_t, map_all, all_map, picked, slot_rows, spread,
    loads, solution, basis, weight, residual, field, local, early, both, edge_both, term_both, sol_both, coarse_rows, corrected,
    faces, arrived, term_all, sol_all,
    load_sem, out_sem, map_send, map_recv, face_send, face_recv, term_send, term_recv, sol_send, sol_recv,
):
    grid = Grid(sizes)
    unknowns, cases = solution.shape
    primal = basis.shape[1]
    own = coarse_t.shape[1]
    edge = corrected.shape[0]
    shape_turn = 2
    first_own = pl.multiple_of(grid.c[2] * own, own)

    def load(k, source, target):
        return pltpu.make_async_copy(source, target, load_sem.at[k])

    load_x = load(0, start_in, solution)
    chunk = tile_of(unknowns, 256)
    chunks = unknowns // chunk
    load_s = [
        load(7 + i, schur.at[pl.ds(i * chunk, chunk)], full.at[pl.ds(i * chunk, chunk)]) for i in range(chunks)
    ]
    load_m = load(2, basis_in, basis)
    load_l = load(3, loads_in, loads)
    load_c = load(4, coarse_inv.at[pl.ds(first_own, own)], coarse_own)
    load_b = load(5, inverse, full)
    load_i = [
        load(7 + chunks, lists_in, slots), load(8 + chunks, lists_in, slot_lists),
        load(9 + chunks, multiplicity_in, multiplicity),
    ]
    me = grid.linear(grid.place)
    load_o = load(10 + chunks, own_map_in, map_all.at[me])
    for each in (load_x, *load_s, *load_i, load_o, load_m, load_l, load_c):
        each.start()
    for landing in arrived:
        landing[...] = jnp.zeros_like(landing)
    with jax.named_scope("announce"):
        grid.announce()

    with jax.named_scope("splitx"):
        load_x.wait()
        split_beside(solution, both)

    def stiff(r):
        field[r, :] = product(s_high[r, :], s_low[r, :], both)

    with jax.named_scope("stiff0"):
        for i in range(chunks):
            r = pl.ds(i * chunk, chunk)
            load_s[i].wait()
            split_rows(full.at[r], s_high.at[r], s_low.at[r])
            stiff(r)
    load_b.start()

    def face_copy(turn, d):
        axis, side = d // 2, d % 2
        target = list(grid.c)
        target[axis] = grid.c[axis] + (1 if side else -1)
        return pltpu.make_async_remote_copy(
            src_ref=faces.at[turn, pl.ds(d * face, face)],
            dst_ref=arrived[turn].at[pl.ds((d ^ 1) * face, face)],
            send_sem=face_send.at[turn, d],
            recv_sem=face_recv.at[turn, d ^ 1],
            device_id=tuple(target), device_id_type=MESH,
        )

    def exists(d):
        axis, side = d // 2, d % 2
        return grid.c[axis] < sizes[axis] - 1 if side else grid.c[axis] > 0

    def collect(turn, source, d):
        take_rows(faces.at[turn, pl.ds(d * face, face)], source, slots.at[d, 0], face)

    def dispatch(turn, d):
        @pl.when(exists(d))
        def _():
            face_copy(turn, d).start()

    def exchange_start(turn, source):
        for d in range(6):
            collect(turn, source, d)
            dispatch(turn, d)

    def exchange_wait(turn):
        for d in range(6):

            @pl.when(exists(d))
            def _():
                block = arrived[turn].at[pl.ds(d * face, face)]
                pltpu.make_async_remote_copy(
                    src_ref=block, dst_ref=block, send_sem=face_send.at[turn, d],
                    recv_sem=face_recv.at[turn, d], device_id=grid.c, device_id_type=MESH,
                ).wait_recv()

    def exchange_drain(turn):
        for d in range(6):

            @pl.when(exists(d))
            def _():
                face_copy(turn, d).wait_send()

    with jax.named_scope("collect"):
        for each in (*load_i, load_o):
            each.wait()
        collect(0, field, 0)
    with jax.named_scope("meet"):
        grid.meet()
    with jax.named_scope("xstart"):
        dispatch(0, 0)
        for d in range(1, 6):
            collect(0, field, d)
            dispatch(0, d)
    with jax.named_scope("mapsend"):

        def map_copy(target):
            return pltpu.make_async_remote_copy(
                src_ref=map_all.at[me], dst_ref=map_all.at[me], send_sem=map_send, recv_sem=map_recv,
                device_id=target, device_id_type=MESH,
            )

        grid.others(lambda target: map_copy(target).start())
    with jax.named_scope("basis"):
        load_m.wait()
        for k in range(0, unknowns, 128):
            r = slice(k, k + 128)
            inverse_count = 1.0 / multiplicity[:, r].astype(jnp.float32)
            weight[r, :] = jnp.broadcast_to(inverse_count, (cases, 128)).T
            scaled = weight[r, 0:1] * basis[r, :]
            basis[r, :] = scaled
            h, l = split(scaled)
            m_high[r, :] = h
            m_low[r, :] = l
            h, l = split(scaled.T)
            t_high[:, r] = h
            t_low[:, r] = l
    with jax.named_scope("psi"):
        for d in range(6):
            collect(shape_turn, basis, d)
        shape_edges = faces.at[shape_turn]
        if edge > 6 * face:
            shape_edges[6 * face : edge, :] = jnp.zeros((edge - 6 * face, cases), jnp.float32)
        for k in range(0, edge, 128):
            h, l = split(shape_edges[k : k + 128, :].T)
            p_high[:, k : k + 128] = h
            p_low[:, k : k + 128] = l
    for d in range(6):
        dispatch(shape_turn, d)

    def moved(r):
        wide = jnp.dot(spread[r, :], edge_both[...], preferred_element_type=jnp.float32)
        return wide[:, 0:cases] + wide[:, cases : 2 * cases]

    def neighbour(d):
        axis, side = d // 2, d % 2
        stride = (sizes[1] * sizes[2], sizes[2], 1)[axis]
        step = (grid.c[axis] + (1 if side else -1) + sizes[axis]) % sizes[axis] - grid.c[axis]
        return me + step * stride

    to_scalars = pltpu.make_async_copy(map_all, all_map, load_sem.at[6])
    gathers = []
    for iteration in range(ITERS):
        turn = 0
        slot = iteration % term_all.shape[0]
        if iteration:
            with jax.named_scope("splitx"):
                split_beside(solution, both)
            with jax.named_scope("stiff"):
                by_rows(unknowns, 256, stiff)
            with jax.named_scope("xstart"):
                for old in (0, 1):
                    exchange_drain(old)
                for gather in gathers:
                    gather.drain()
                gathers = []
                exchange_start(turn, field)
        else:
            load_l.wait()

        def before(r):
            value = loads[r, :] - field[r, :]
            field[r, :] = value
            h, l = split(value)
            both[r, 0:cases] = h
            both[r, cases : 2 * cases] = l

        with jax.named_scope("before"):
            by_rows(unknowns, 128, before)
            early[...] = product(t_high[...], t_low[...], both)
        with jax.named_scope("xwait"):
            exchange_wait(turn)
        with jax.named_scope("term"):
            split_beside(arrived[turn], edge_both)
            mine = pl.multiple_of(me * primal, primal)
            term_all[slot, pl.ds(mine, primal), :] = early[...] - product(p_high[...], p_low[...], edge_both)
        terms = Halves(grid, term_all.at[slot], primal, term_send, term_recv)
        with jax.named_scope("termstart"):
            terms.start()
        gathers.append(terms)

        def settle(r):
            value = field[r, :] - moved(r)
            residual[r, :] = value
            h, l = split(weight[r, :] * value)
            both[r, 0:cases] = h
            both[r, cases : 2 * cases] = l

        if iteration == 0:
            with jax.named_scope("spread"):
                slot_rows[...] = jnp.full(slot_rows.shape, -1, jnp.int32)
                for d in range(6):
                    slot_rows[:, d * face : (d + 1) * face] = slot_lists[d]
                hits = slot_rows[...]
                tile = tile_of(unknowns, 64)

                def mark(i, carry):
                    r = pl.ds(pl.multiple_of(i * tile, tile), tile)
                    row = lax.broadcasted_iota(jnp.int32, (tile, edge), 0) + i * tile
                    spread[r, :] = jnp.where(row == hits, 1.0, 0.0).astype(jnp.bfloat16)
                    return carry

                lax.fori_loop(0, unknowns // tile, mark, 0)
                corrected[...] = jnp.zeros_like(corrected)
        with jax.named_scope("settle"):
            by_rows(unknowns, 256, settle)
        if iteration == ITERS - 1:
            out_residual = pltpu.make_async_copy(residual, residual_out, out_sem.at[0])
            out_residual.start()

        def invert(r):
            local[r, :] = weight[r, :] * product(b_high[r, :], b_low[r, :], both)

        def inverts(i):
            def run():
                with jax.named_scope("invert"):
                    invert(pl.ds(i * chunk, chunk))

            return run

        def splits(i):
            def run():
                with jax.named_scope("splitb"):
                    if i == 0:
                        load_b.wait()
                    r = pl.ds(i * chunk, chunk)
                    split_rows(full.at[r], b_high.at[r], b_low.at[r])

            return run

        def turn_coarse():
            with jax.named_scope("transc"):
                load_c.wait()
                for k in range(0, coarse_own.shape[1], 128):
                    coarse_t[k : k + 128, :] = coarse_own[:, k : k + 128].T

        def read_maps():
            with jax.named_scope("maps"):
                if grid.count > 1:
                    block = map_all.at[pl.ds(0, grid.count - 1)]
                    pltpu.make_async_remote_copy(
                        src_ref=block, dst_ref=block, send_sem=map_send, recv_sem=map_recv,
                        device_id=grid.c, device_id_type=MESH,
                    ).wait()
                to_scalars.start()

        def pick(p, carry):
            take_rows(picked, coarse_t, all_map.at[p, 0], primal)
            h, l = split(picked[...].T)
            k = pl.ds(pl.multiple_of(p * primal, primal), primal)
            c_high[:, k] = h
            c_low[:, k] = l
            return carry

        plane = grid.count // sizes[0]
        width = plane * primal
        coarse_tile = term_both.shape[0]
        mine = pl.multiple_of(me * own, own)
        sol_all[iteration][pl.ds(mine, own), :] = jnp.zeros((own, cases), jnp.float32)

        def plane_of(head):
            return (grid.c[0] + sizes[0] - head) % sizes[0]

        def picks(head, part, parts):
            def run():
                with jax.named_scope("pick"):
                    if head == 0 and part == 0:
                        to_scalars.wait()
                    first = plane_of(head) * plane
                    lax.fori_loop(first + plane * part // parts, first + plane * (part + 1) // parts, pick, 0)

            return run

        def collects(d):
            def run():
                with jax.named_scope("clocal"):
                    collect(1, local, d)

            return run

        if iteration == 0:
            read_maps()
            first = [turn_coarse] + [picks(head, part, 4) for head in range(sizes[0]) for part in range(4)]
            work = [splits(i) for i in range(chunks)]
        else:
            first, work = [], []
        work += [inverts(i) for i in range(chunks)] + [collects(d) for d in range(6)]

        def after_plane(head):
            def coarse(i, carry):
                k = pl.ds(pl.multiple_of(plane_of(head) * width + i * coarse_tile, coarse_tile), coarse_tile)
                split_beside(term_all.at[slot, k], term_both)
                sol_all[iteration][pl.ds(mine, own), :] += product(c_high[:, k], c_low[:, k], term_both)
                return carry

            with jax.named_scope("coarse"):
                lax.fori_loop(0, width // coarse_tile, coarse, 0)

        with jax.named_scope("termfin"):
            terms.finish(first, work, after_plane)
        sols = Halves(grid, sol_all[iteration], own, sol_send, sol_recv)
        with jax.named_scope("solstart"):
            sols.start()
        gathers.append(sols)

        with jax.named_scope("xlocal"):
            for d in range(6):
                dispatch(1, d)

        def approach(r):
            solution[r, :] = solution[r, :] + damping * (local[r, :] + moved(r))

        def approaches(i):
            def run():
                with jax.named_scope("approach"):
                    if i == 0:
                        exchange_wait(1)
                        split_beside(arrived[1], edge_both)
                    approach(pl.ds(i * chunk, chunk))

            return run

        def shapes():
            with jax.named_scope("shapes"):
                exchange_wait(shape_turn)
                split_rows(arrived[shape_turn], n_high, n_low)

        nothing = [lambda: None] * (2 * (sum(grid.stages[:1]) - 1))
        work = ([shapes] if iteration == 0 else []) + nothing + [approaches(i) for i in range(chunks)]
        with jax.named_scope("solfin"):
            sols.finish((), work)
        with jax.named_scope("take"):
            take_rows(coarse_rows, sol_all[iteration], all_map.at[me, 0], primal)
            split_beside(coarse_rows, sol_both)
            for d in range(6):

                @pl.when(exists(d))
                def _():
                    q = neighbour(d)
                    r = slice(d * face, (d + 1) * face)
                    take_rows(coarse_rows, sol_all[iteration], all_map.at[q, 0], primal)
                    split_beside(coarse_rows, term_both.at[0:primal])
                    corrected[r, :] = product(n_high[r, :], n_low[r, :], term_both.at[0:primal])

            split_beside(corrected, edge_both)

        def advance(r):
            change = product(m_high[r, :], m_low[r, :], sol_both) + moved(r)
            solution[r, :] = solution[r, :] + damping * change

        with jax.named_scope("advance"):
            by_rows(unknowns, 256, advance)
    with jax.named_scope("out"):
        out_solution = pltpu.make_async_copy(solution, solution_out, out_sem.at[1])
        out_solution.start()
        for turn in range(3):
            exchange_drain(turn)
        for gather in gathers:
            gather.drain()
        out_residual.wait()
        out_solution.wait()


def body(sizes, loads, start, schur, inv_local, basis, coarse_inv, face_index, multiplicity, primal_map):
    unknowns, cases = loads.shape[3:]
    face = face_index.shape[4]
    primal = basis.shape[4]
    count = sizes[0] * sizes[1] * sizes[2]
    total = coarse_inv.shape[1]
    own = coarse_inv.shape[0] // sizes[2]
    edge = -(-6 * face // 128) * 128
    anywhere = pl.BlockSpec(memory_space=pl.ANY)
    dma = pltpu.SemaphoreType.DMA
    f32, bf16 = jnp.float32, jnp.bfloat16
    turns = 3
    coarse_tile = tile_of(count // sizes[0] * primal, 1024)
    grid_stages = stages_of(sizes)
    landings = max(arrivals(grid_stages), arrivals((grid_stages[0], grid_stages[2], grid_stages[1], grid_stages[3])))
    term_slots = ITERS if ITERS * count * primal <= 8 * unknowns else 1
    vec = pltpu.VMEM((unknowns, cases), f32)
    out = jax.ShapeDtypeStruct((unknowns, cases), f32)
    lists = face_index.reshape(6, 1, face)
    solution, residual = pl.pallas_call(
        functools.partial(main_kernel, sizes, face),
        out_shape=(out, out),
        in_specs=[anywhere] * 9,
        out_specs=(anywhere, anywhere),
        scratch_shapes=[
            pltpu.SMEM((6, 1, face), jnp.int32),
            pltpu.VMEM((6, 1, face), jnp.int32),
            pltpu.VMEM((1, unknowns), jnp.int32),
            pltpu.VMEM((unknowns, unknowns), f32),
            pltpu.VMEM((unknowns, unknowns), bf16),
            pltpu.VMEM((unknowns, unknowns), bf16),
            pltpu.VMEM((unknowns, unknowns), bf16),
            pltpu.VMEM((unknowns, unknowns), bf16),
            pltpu.VMEM((unknowns, primal), bf16),
            pltpu.VMEM((unknowns, primal), bf16),
            pltpu.VMEM((primal, unknowns), bf16),
            pltpu.VMEM((primal, unknowns), bf16),
            pltpu.VMEM((primal, edge), bf16),
            pltpu.VMEM((primal, edge), bf16),
            pltpu.VMEM((edge, primal), bf16),
            pltpu.VMEM((edge, primal), bf16),
            pltpu.VMEM((own, count * primal), bf16),
            pltpu.VMEM((own, count * primal), bf16),
            pltpu.VMEM((own, total), f32),
            pltpu.VMEM((total, own), f32),
            pltpu.VMEM((count, 1, primal), jnp.int32),
            pltpu.SMEM((count, 1, primal), jnp.int32),
            pltpu.VMEM((primal, own), f32),
            pltpu.VMEM((1, edge), jnp.int32),
            pltpu.VMEM((unknowns, edge), bf16),
            vec, vec, pltpu.VMEM((unknowns, primal), f32), vec, vec, vec, vec,
            pltpu.VMEM((primal, cases), f32),
            pltpu.VMEM((unknowns, 2 * cases), bf16),
            pltpu.VMEM((edge, 2 * cases), bf16),
            pltpu.VMEM((coarse_tile, 2 * cases), bf16),
            pltpu.VMEM((primal, 2 * cases), bf16),
            pltpu.VMEM((primal, cases), f32),
            pltpu.VMEM((edge, cases), f32),
            pltpu.VMEM((turns, edge, cases), f32),
            [pltpu.VMEM((edge, cases), f32) for _ in range(turns)],
            pltpu.VMEM((term_slots, count * primal, cases), f32),
            [pltpu.VMEM((total, cases), f32) for _ in range(ITERS)],
            dma((11 + unknowns // tile_of(unknowns, 256),)), dma((2,)),
            dma(()), dma(()),
            dma((turns, 6)), dma((turns, 6)),
            dma((2,)), dma((2, landings)),
            dma((2,)), dma((2, landings)),
        ],
        compiler_params=pltpu.CompilerParams(
            collective_id=1, has_side_effects=True, vmem_limit_bytes=67043328
        ),
    )(
        lists, multiplicity.reshape(1, unknowns), primal_map.reshape(1, primal),
        loads.reshape(unknowns, cases), start.reshape(unknowns, cases), basis.reshape(unknowns, primal),
        schur.reshape(unknowns, unknowns), inv_local.reshape(unknowns, unknowns), coarse_inv,
    )
    return (solution.reshape(loads.shape), residual.reshape(loads.shape))


def solution(mesh):
    sizes = tuple(mesh.shape[a] for a in AXES)
    field = P("gx", "gy", "gz", None, None)
    placed = (field,) * 5 + (P(("gx", "gy"), None), field, P("gx", "gy", "gz", None), P("gx", "gy", "gz", None))
    return jax.shard_map(
        functools.partial(body, sizes),
        mesh=mesh,
        in_specs=placed,
        out_specs=(field, field),
        check_vma=False,
    )
```

time: 118 us -> 98.7 us (0.84)
  Pallas kernels: 111 us -> 94.1 us
  local copies, waits for them, and re-layouts: 5.71 us -> 3.74 us
    pallas_call x1, Pallas kernels: 111 us -> 94.1 us  [body(): pl.pallas_call(functools.partial(main_kernel, sizes, face), out_shape=(ou...]
    unnamed x3 -> x2, local copies, waits for them, and re-layouts: 5.03 us -> 3.74 us
where the time goes in v2:
time: 98.7 us; the launch traced here: 98.5 us
  Pallas kernels  94.1 us (95%)
  local copies, waits for them, and re-layouts  3.74 us (4%)
    pallas_call x1, Pallas kernels, body(): pl.pallas_call(functools.partial(main_kernel, sizes, face), out_shape=(ou...  94.1 us
    unnamed x2, local copies, waits for them, and re-layouts  3.74 us

profile of v2, /device:TPU:1, one launch (start us, length us, event | category | flops | bytes accessed | tf_op | source)
XLA Modules:
  0.0 98.5 jit_solution(17573482762945031337)
XLA Ops:
  0.6 94.1 %shard_map.104 = (f32[1024,128]{1,0:T(8,128)}, f32[1024,128]{1,0:T(8,128)}) custom-call(s32[6,1,160]{2,1,0:T(1,128)} %bitcast.17, s32[1,1024]{1,0:T(1,128)} %bitcast.18, s32[1,128]{1,0:T(1,128)} %bitcast.19, f32[1024,128]{1,0:T(8,128)} %bitcast.14, f32[1024,128]{1,0:T(8,128)} %bitcast.15, f32[1024,128]{1,0:T(8,128)} %bitcast.16, f32[1024,1024]{1,0:T(8,128)} %bitcast.10, ...), custom_call_target="tpu_custom_call" | custom-call | tf_op jit(solution)/shard_map/pallas_call | solution.py:654
  94.8 1.9 %copy.13 = f32[1,1,1,1024,128]{4,3,2,1,0:T(8,128)} copy(f32[1,1,1,1024,128]{4,3,2,1,0:T(8,128)} %bitcast.13) | data formatting | bytes 1048576
  96.7 1.9 %copy.14 = f32[1,1,1,1024,128]{4,3,2,1,0:T(8,128)} copy(f32[1,1,1,1024,128]{4,3,2,1,0:T(8,128)} %bitcast.12) | data formatting | bytes 1048576

commit v3 on v2

--- a/solution.py
+++ b/solution.py
@@ -29,6 +29,14 @@
         self.count = gx * gy * gz
         self.c = tuple(lax.axis_index(a) for a in AXES)
         self.place = (self.c[0], self.c[1], self.c[2] // self.lo, self.c[2] % self.lo)
+        z = self.c[0]
+        if gx == 4:
+            inner = (z % 3 + 1) // 2
+            self.line = (z, z + 1 - 2 * (z % 2), 2 - z // 2, 3 - 3 * (z // 2))
+            self.back = (0, 1, 3 - inner, 3 - inner)
+        else:
+            self.line = tuple((z + gx - d) % gx for d in range(gx))
+            self.back = tuple((gx - d) % gx for d in range(gx))
 
     def linear(self, place):
         x, y, h, l = place
@@ -66,7 +74,9 @@
         g = self.grid
         place = list(g.place)
         for o, d in zip(self.order, offset):
-            if d:
+            if o == 0:
+                place[0] = g.line[d]
+            elif d:
                 place[o] = (g.place[o] + g.stages[o] - d) % g.stages[o]
         return place
 
@@ -92,9 +102,10 @@
         for stage in range(first, 4):
             for delta in range(1, self.lengths[stage]):
                 back = [0, 0, 0, 0]
-                back[stage] = self.lengths[stage] - delta
+                back[stage] = delta
                 arrived = list(offset)
-                arrived[stage] = delta
+                axis = self.order[stage]
+                arrived[stage] = self.grid.back[delta] if axis == 0 else self.lengths[stage] - delta
                 self.copy(
                     self.block(offset), self.number(arrived), self.grid.device(self.place(back))
                 ).start()
@@ -102,12 +113,12 @@
     def start(self):
         self.forward((0, 0, 0, 0), 0)
 
-    def finish(self, stage, heads=None, idle=None):
-        for head in itertools.product(*[range(n) for n in self.lengths[:stage]]):
-            if heads is not None and head[0] != heads:
-                continue
+    def finish(self, stage, head, idle=None):
+        for rest in itertools.product(*[range(n) for n in self.lengths[:stage]]):
             for delta in range(1, self.lengths[stage]):
-                arrived = tuple(head) + (delta,) + (0,) * (3 - stage)
+                arrived = tuple(rest) + (delta,) + (0,) * (3 - stage)
+                if arrived[0] != head:
+                    continue
                 self.copy(self.block(arrived), self.number(arrived), self.grid.c).wait_recv()
                 self.forward(arrived, stage + 1)
                 if idle:
@@ -143,6 +154,15 @@
         for part in self.parts:
             part.start()
 
+    def waits(self, stages):
+        total = 0
+        for part in self.parts:
+            ahead = 1
+            for n in part.lengths[:stages]:
+                total += ahead * (n - 1)
+                ahead *= n
+        return total
+
     def finish(self, first=(), work=(), after=None):
         first, work = list(first), list(work)
 
@@ -151,8 +171,9 @@
                 (first or work).pop(0)()
 
         for stage in range(2):
-            for part in self.parts:
-                part.finish(stage, None, idle)
+            for head in range(self.heads):
+                for part in self.parts:
+                    part.finish(stage, head, idle)
 
         def close(head):
             for part in self.parts:
@@ -243,6 +264,10 @@
         return carry
 
     lax.fori_loop(0, count // unroll, step, 0)
+
+
+def pause():
+    pass
 
 
 def main_kernel(
@@ -410,13 +435,17 @@
         return me + step * stride
 
     to_scalars = pltpu.make_async_copy(map_all, all_map, load_sem.at[6])
+    out_solution = [
+        pltpu.make_async_copy(
+            solution.at[pl.ds(i * chunk, chunk)], solution_out.at[pl.ds(i * chunk, chunk)], out_sem.at[1 + i]
+        )
+        for i in range(chunks)
+    ]
     gathers = []
     for iteration in range(ITERS):
         turn = 0
         slot = iteration % term_all.shape[0]
         if iteration:
-            with jax.named_scope("splitx"):
-                split_beside(solution, both)
             with jax.named_scope("stiff"):
                 by_rows(unknowns, 256, stiff)
             with jax.named_scope("xstart"):
@@ -530,7 +559,7 @@
         sol_all[iteration][pl.ds(mine, own), :] = jnp.zeros((own, cases), jnp.float32)
 
         def plane_of(head):
-            return (grid.c[0] + sizes[0] - head) % sizes[0]
+            return grid.line[head]
 
         def picks(head, part, parts):
             def run():
@@ -555,6 +584,11 @@
             work = [splits(i) for i in range(chunks)]
         else:
             first, work = [], []
+        def send_local():
+            with jax.named_scope("xlocal"):
+                for d in range(6):
+                    dispatch(1, d)
+
         work += [inverts(i) for i in range(chunks)] + [collects(d) for d in range(6)]
 
         def after_plane(head):
@@ -574,9 +608,7 @@
             sols.start()
         gathers.append(sols)
 
-        with jax.named_scope("xlocal"):
-            for d in range(6):
-                dispatch(1, d)
+        send_local()
 
         def approach(r):
             solution[r, :] = solution[r, :] + damping * (local[r, :] + moved(r))
@@ -596,8 +628,7 @@
                 exchange_wait(shape_turn)
                 split_rows(arrived[shape_turn], n_high, n_low)
 
-        nothing = [lambda: None] * (2 * (sum(grid.stages[:1]) - 1))
-        work = ([shapes] if iteration == 0 else []) + nothing + [approaches(i) for i in range(chunks)]
+        work = ([shapes] if iteration == 0 else []) + [pause] * sols.waits(1) + [approaches(i) for i in range(chunks)]
         with jax.named_scope("solfin"):
             sols.finish((), work)
         with jax.named_scope("take"):
@@ -617,19 +648,48 @@
 
         def advance(r):
             change = product(m_high[r, :], m_low[r, :], sol_both) + moved(r)
-            solution[r, :] = solution[r, :] + damping * change
+            value = solution[r, :] + damping * change
+            solution[r, :] = value
+            if iteration < ITERS - 1:
+                h, l = split(value)
+                both[r, 0:cases] = h
+                both[r, cases : 2 * cases] = l
 
         with jax.named_scope("advance"):
-            by_rows(unknowns, 256, advance)
+            if iteration < ITERS - 1:
+                by_rows(unknowns, 256, advance)
+            else:
+                for i in range(chunks):
+                    r = pl.ds(i * chunk, chunk)
+                    advance(r)
+                    out_solution[i].start()
     with jax.named_scope("out"):
-        out_solution = pltpu.make_async_copy(solution, solution_out, out_sem.at[1])
-        out_solution.start()
         for turn in range(3):
             exchange_drain(turn)
         for gather in gathers:
             gather.drain()
         out_residual.wait()
-        out_solution.wait()
+        for each in out_solution:
+            each.wait()
+
+
+def settle_outputs(first_in, second_in, first_out, second_out, stage, come, go):
+    pairs = ((first_in, first_out), (second_in, second_out))
+    pieces = stage.shape[1]
+    rows = stage.shape[2]
+    entering, leaving = [], []
+    for i in range(pieces):
+        for k, (source, target) in enumerate(pairs):
+            r = pl.ds(i * rows, rows)
+            entering.append(pltpu.make_async_copy(source.at[r], stage.at[k, i], come.at[k, i]))
+            leaving.append(pltpu.make_async_copy(stage.at[k, i], target.at[r], go.at[k, i]))
+    for each in entering:
+        each.start()
+    for a, b in zip(entering, leaving):
+        a.wait()
+        b.start()
+    for each in leaving:
+        each.wait()
 
 
 def body(sizes, loads, start, schur, inv_local, basis, coarse_inv, face_index, multiplicity, primal_map):
@@ -694,7 +754,7 @@
             [pltpu.VMEM((edge, cases), f32) for _ in range(turns)],
             pltpu.VMEM((term_slots, count * primal, cases), f32),
             [pltpu.VMEM((total, cases), f32) for _ in range(ITERS)],
-            dma((11 + unknowns // tile_of(unknowns, 256),)), dma((2,)),
+            dma((11 + unknowns // tile_of(unknowns, 256),)), dma((1 + unknowns // tile_of(unknowns, 256),)),
             dma(()), dma(()),
             dma((turns, 6)), dma((turns, 6)),
             dma((2,)), dma((2, landings)),
@@ -708,6 +768,15 @@
         loads.reshape(unknowns, cases), start.reshape(unknowns, cases), basis.reshape(unknowns, primal),
         schur.reshape(unknowns, unknowns), inv_local.reshape(unknowns, unknowns), coarse_inv,
     )
+    pieces = 2
+    rows = unknowns // pieces
+    solution, residual = pl.pallas_call(
+        settle_outputs,
+        out_shape=(out, out),
+        in_specs=[anywhere] * 2,
+        out_specs=(anywhere, anywhere),
+        scratch_shapes=[pltpu.VMEM((2, pieces, rows, cases), f32), dma((2, pieces)), dma((2, pieces))],
+    )(solution, residual)
     return (solution.reshape(loads.shape), residual.reshape(loads.shape))
 
 

time: 98.7 us -> 95.2 us (0.965)
  local copies, waits for them, and re-layouts: 3.74 us -> 0 us
    unnamed x2 -> x0, local copies, waits for them, and re-layouts: 3.74 us -> none
    pallas_call x0 -> x1, Pallas kernels: none -> 1.98 us  [body(): pl.pallas_call(settle_outputs, out_shape=(out, out), in_specs=[anywhere]...]
    pallas_call x1, Pallas kernels: 94.1 us -> 92.3 us  [body(): pl.pallas_call(functools.partial(main_kernel, sizes, face), out_shape=(ou...]
where the time goes in v3:
time: 95.2 us; the launch traced here: 95.1 us
  Pallas kernels  94.3 us (99%)
    pallas_call x1, Pallas kernels, body(): pl.pallas_call(functools.partial(main_kernel, sizes, face), out_shape=(ou...  92.3 us
    pallas_call x1, Pallas kernels, body(): pl.pallas_call(settle_outputs, out_shape=(out, out), in_specs=[anywhere]...  1.98 us

profile of v3, /device:TPU:1, one launch (start us, length us, event | category | flops | bytes accessed | tf_op | source)
XLA Modules:
  0.0 95.1 jit_solution(13364074985441459588)
XLA Ops:
  0.6 92.3 %shard_map.104 = (f32[1024,128]{1,0:T(8,128)}, f32[1024,128]{1,0:T(8,128)}) custom-call(s32[6,1,160]{2,1,0:T(1,128)} %bitcast.15, s32[1,1024]{1,0:T(1,128)} %bitcast.16, s32[1,128]{1,0:T(1,128)} %bitcast.17, f32[1024,128]{1,0:T(8,128)} %bitcast.12, f32[1024,128]{1,0:T(8,128)} %bitcast.13, f32[1024,128]{1,0:T(8,128)} %bitcast.14, f32[1024,1024]{1,0:T(8,128)} %bitcast.10, ...), custom_call_target="tpu_custom_call" | custom-call | tf_op jit(solution)/shard_map/pallas_call | solution.py:714
  92.9 2.0 %shard_map.105 = (f32[1024,128]{1,0:T(8,128)}, f32[1024,128]{1,0:T(8,128)}) custom-call(f32[1024,128]{1,0:T(8,128)} %get-tuple-element.6.first_in, f32[1024,128]{1,0:T(8,128)} %get-tuple-element.7.second_in), custom_call_target="tpu_custom_call" | custom-call | tf_op jit(solution)/shard_map/pallas_call | solution.py:773

commit v4 on v3

--- a/solution.py
+++ b/solution.py
@@ -255,7 +255,7 @@
 
 
 def take_rows(target, source, index, count):
-    unroll = tile_of(count, 32)
+    unroll = tile_of(count, 64)
 
     def step(i, carry):
         first = pl.multiple_of(i * unroll, unroll)
@@ -447,7 +447,7 @@
         slot = iteration % term_all.shape[0]
         if iteration:
             with jax.named_scope("stiff"):
-                by_rows(unknowns, 256, stiff)
+                by_rows(unknowns, 512, stiff)
             with jax.named_scope("xstart"):
                 for old in (0, 1):
                     exchange_drain(old)
@@ -503,7 +503,7 @@
                 lax.fori_loop(0, unknowns // tile, mark, 0)
                 corrected[...] = jnp.zeros_like(corrected)
         with jax.named_scope("settle"):
-            by_rows(unknowns, 256, settle)
+            by_rows(unknowns, 512, settle)
         if iteration == ITERS - 1:
             out_residual = pltpu.make_async_copy(residual, residual_out, out_sem.at[0])
             out_residual.start()
@@ -657,7 +657,7 @@
 
         with jax.named_scope("advance"):
             if iteration < ITERS - 1:
-                by_rows(unknowns, 256, advance)
+                by_rows(unknowns, 512, advance)
             else:
                 for i in range(chunks):
                     r = pl.ds(i * chunk, chunk)

time: 95.2 us -> 94.7 us (level)
  no operation moved by 1% of the time
where the time goes in v4:
time: 94.7 us; the launch traced here: 94.6 us
  Pallas kernels  93.8 us (99%)
    pallas_call x1, Pallas kernels, body(): pl.pallas_call(functools.partial(main_kernel, sizes, face), out_shape=(ou...  91.8 us
    pallas_call x1, Pallas kernels, body(): pl.pallas_call(settle_outputs, out_shape=(out, out), in_specs=[anywhere]...  1.98 us

profile of v4, /device:TPU:1, one launch (start us, length us, event | category | flops | bytes accessed | tf_op | source)
XLA Modules:
  0.0 94.6 jit_solution(7750447082947655126)
XLA Ops:
  0.6 91.8 %shard_map.104 = (f32[1024,128]{1,0:T(8,128)}, f32[1024,128]{1,0:T(8,128)}) custom-call(s32[6,1,160]{2,1,0:T(1,128)} %bitcast.15, s32[1,1024]{1,0:T(1,128)} %bitcast.16, s32[1,128]{1,0:T(1,128)} %bitcast.17, f32[1024,128]{1,0:T(8,128)} %bitcast.12, f32[1024,128]{1,0:T(8,128)} %bitcast.13, f32[1024,128]{1,0:T(8,128)} %bitcast.14, f32[1024,1024]{1,0:T(8,128)} %bitcast.10, ...), custom_call_target="tpu_custom_call" | custom-call | tf_op jit(solution)/shard_map/pallas_call | solution.py:714
  92.4 2.0 %shard_map.105 = (f32[1024,128]{1,0:T(8,128)}, f32[1024,128]{1,0:T(8,128)}) custom-call(f32[1024,128]{1,0:T(8,128)} %get-tuple-element.6.first_in, f32[1024,128]{1,0:T(8,128)} %get-tuple-element.7.second_in), custom_call_target="tpu_custom_call" | custom-call | tf_op jit(solution)/shard_map/pallas_call | solution.py:773
